TPU v7x, 32 devices: a whole 2x2x4 slice. The times are simulated.
32 devices in a mesh: parts: 2 (over x), loop: 4 (over y, core), tgrp: 4 (over z).
Axes of the slice: x: 2, y: 2, z: 4, core: 2. Of those that a mesh axis runs over, the one named last changes fastest.
Arguments:
- data: bfloat16 [8, 3, 12288], P(('parts', 'loop'), None, 'tgrp'), parts along dimension 0
- templates: bfloat16 [128, 4, 3, 2048], P('tgrp', 'loop')
- masks: int32 [128, 4], replicated, may hold values from 0 to 1, as said below
- offsets: int32 [8], P(('parts', 'loop')), parts along dimension 0, may hold values from 0 to 512, as said below
- active: int32 [8, 3], P(('parts', 'loop')), parts along dimension 0, may hold values 0 or 1
Outputs:
- detection: float32 [256, 12288], P(('parts', 'loop'), 'tgrp'), parts along dimension 0
There are 2 independent parts, one for each index of `parts`. A program takes and returns all parts, laid end to end along the dimension named above; an argument that names none is the same for every part. Nothing has to cross between parts.
Inputs may be any that keep to these rules, and one draw needn't show every extreme that they name: `masks`: every template uses at least one station. `offsets`: some station has an offset of exactly 512.
All inputs are finite; a program needn't handle non-finite values. No bound on the sum of `active` on one device may be relied on, other than what follows from the above.
Results may differ from a plain program's by a relative error of at most 0.0003.
Values may be sent and summed in bfloat16 or wider, within the bound.
No kernel may reach another device: no remote copies, remote signals or barrier semaphores. Data moves between devices by JAX's collectives and lax.ppermute only.
A program may use at most 64 MiB of HBM per device.

v0:
```python
import jax
import jax.numpy as jnp
from jax import lax
from jax.sharding import PartitionSpec as P

L = 2048
epsilon = 1e-05


def passed_along(value, axis, steps):
    count = lax.axis_size(axis)
    initial, last = (max(0, -steps), min(count, count - steps))
    return lax.ppermute(value, axis, [(source, source + steps) for source in range(initial, last)])


def window_energy(squares, out_len, span):
    inner_len = out_len + span - 128
    nblocks = (inner_len + 127) // 128
    total_len = 128 * (nblocks + 1)
    padded = jnp.concatenate([squares, jnp.zeros((total_len - squares.shape[0],), squares.dtype)])
    first = padded[: 128 * nblocks].reshape(nblocks, 128)
    second = padded[128 : 128 * nblocks + 128].reshape(nblocks, 128)
    segments = jnp.concatenate([first, second], axis=1)
    rows_at = lax.broadcasted_iota(jnp.int32, (256, 128), 0)
    cols_at = lax.broadcasted_iota(jnp.int32, (256, 128), 1)
    gap = rows_at - cols_at
    band = jnp.where((gap >= 0) & (gap < 128), 1.0, 0.0).astype(squares.dtype)
    inner = jnp.dot(segments, band, precision=lax.Precision.HIGHEST).reshape(nblocks * 128)
    energy = jnp.zeros((out_len,), squares.dtype)
    for block_at in range(span // 128):
        energy = energy + inner[128 * block_at : 128 * block_at + out_len]
    return energy


def correlate(panel, window, out_len):
    row_count = panel.shape[0]
    blocks = panel.shape[2] // 128
    span_len = out_len + panel.shape[2] - 128
    unfold = jnp.stack(
        [window[:, shift_by : shift_by + span_len] for shift_by in range(128)], axis=1
    )
    unfold = unfold.reshape(3 * 128, span_len)
    frames = (
        panel.reshape(row_count, 3, blocks, 128)
        .transpose(0, 2, 1, 3)
        .reshape(row_count, blocks, 3 * 128)
    )

    def add_block(block_at, running_sum):
        start_at = (block_at * 128).astype(jnp.int32)
        columns = lax.dynamic_slice_in_dim(unfold, start_at, out_len, 1)
        weights_now = lax.dynamic_index_in_dim(frames, block_at, 1, keepdims=False)
        return running_sum + jnp.dot(weights_now, columns, preferred_element_type=jnp.float32)

    return lax.fori_loop(0, blocks, add_block, jnp.zeros((row_count, out_len), jnp.float32))


def local(data, templates, masks, offsets, active):
    local_count = data.shape[0]
    block_len = data.shape[2]
    following = passed_along(data, "tgrp", -1)
    extended = jnp.concatenate([data, following], axis=2)
    loop_at = lax.axis_index("loop")
    first_station = loop_at * local_count
    counts = jnp.sum(masks, axis=1).astype(jnp.float32)
    local_masks = lax.dynamic_slice_in_dim(masks, first_station, local_count, 1)
    weights = local_masks.astype(jnp.float32) * jnp.sqrt(3.0 * L / counts)[:, None]
    station = 0
    channel_on = active[station].astype(jnp.bfloat16)
    series = lax.dynamic_slice(
        extended[station], (jnp.int32(0), offsets[station]), (3, block_len + L)
    )
    window = series * channel_on[:, None]
    wide_window = window.astype(jnp.float32)
    squares = jnp.sum(wide_window * wide_window, axis=0)
    energy = window_energy(squares, block_len, L)
    inv_datas = [1.0 / jnp.sqrt(energy / (3.0 * L) + epsilon)]
    windows = [window]
    channel_sets = [channel_on]
    panel_rows = lax.all_gather(templates, "tgrp", axis=0, tiled=True)
    station = 0
    panel = panel_rows[:, station] * channel_sets[station][None, :, None]
    wide_panel = panel.astype(jnp.float32)
    inv_template = 1.0 / jnp.sqrt(
        jnp.sum(wide_panel * wide_panel, axis=(1, 2)) / (3.0 * L) + epsilon
    )
    corr = correlate(panel, windows[station], block_len)
    row_weights = weights[:, station]
    row_scale = inv_template * row_weights
    stacked = corr * inv_datas[station][None, :] * row_scale[:, None] / (3.0 * L)
    rows_here = stacked.shape[0] // lax.axis_size("loop")
    summed = lax.psum(stacked, "loop")
    return lax.dynamic_slice_in_dim(summed, loop_at * rows_here, rows_here, 0)


def solution(mesh):
    placed = (
        P(("parts", "loop"), None, "tgrp"),
        P("tgrp", "loop", None, None),
        P(),
        P(("parts", "loop")),
        P(("parts", "loop"), None),
    )
    return jax.shard_map(
        local, mesh=mesh, in_specs=placed, out_specs=P(("parts", "loop"), "tgrp"), check_vma=False
    )
```

profile of v0, /device:TPU:0, one launch (start us, length us, event | category | flops | bytes accessed | tf_op | source)
XLA Modules:
  0.0 146.2 jit_solution(8335573352305815033)
XLA Ops:
  6.5 1.3 collective-permute-start
  7.9 0.7 convert_bitcast_fusion
  9.2 0.7 reduce_sum.29
  9.9 3.5 %collective-permute-done = bf16[1,3,3072]{2,1,0:T(4,128)(2,1)S(1)} collective-permute-done((bf16[1,3,3072]{2,1,0:T(4,128)(2,1)}, bf16[1,3,3072]{2,1,0:T(4,128)(2,1)S(1)}, u32[]{:S(2)}, u32[]{:S(2)}) %collective-permute-start) | collective-permute-done | bytes 18464 | tf_op jit(solution)/shard_map/ppermute | solution.py:13
  13.5 0.9 multiply_reduce_fusion.1
  14.4 0.1 constant_dynamic-update-slice_fusion.126
  15.0 0.1 constant_dynamic-update-slice_fusion.121
  15.1 0.1 constant_dynamic-update-slice_fusion.120
  15.3 0.1 constant_dynamic-update-slice_fusion.118
  15.4 0.1 constant_dynamic-update-slice_fusion.117
  15.9 0.1 constant_dynamic-update-slice_fusion.112
  16.1 0.1 constant_dynamic-update-slice_fusion.111
  16.4 0.1 constant_dynamic-update-slice_fusion.108
  16.9 0.1 constant_dynamic-update-slice_fusion.103
  17.7 0.1 constant_dynamic-update-slice_fusion.96
  19.4 0.1 constant_dynamic-update-slice_fusion.80
  21.1 0.1 constant_dynamic-update-slice_fusion.64
  22.8 0.1 constant_dynamic-update-slice_fusion.48
  24.6 0.1 constant_dynamic-update-slice_fusion.32
  28.0 0.1 constant_dynamic-update-slice_fusion
  28.1 2.2 %copy.141 = bf16[3,128,4992]{2,1,0:T(8,128)(2,1)} copy(bf16[3,128,4992]{2,0,1:T(4,128)(2,1)S(1)} %constant_dynamic-update-slice_fusion) | data formatting | bytes 7667712 | tf_op jit(solution)/shard_map/stack | solution.py:39
  30.4 0.2 fusion.4
  30.6 18.2 %all-gather.2.cloned.1.call-done = bf16[128,1,3,2048]{3,0,2,1:T(8,128)(2,1)} async-done(((bf16[32,1,3,2048]{3,0,2,1:T(8,128)(2,1)}), bf16[128,1,3,2048]{3,0,2,1:T(8,128)(2,1)}) %all-gather.2.cloned.1.call-update) | async-done | bytes 1572880 | tf_op jit(solution)/shard_map/all_gather | solution.py:80
  48.9 1.9 %copy.139 = bf16[128,1,3,2048]{0,3,2,1:T(8,128)(2,1)S(1)} copy(bf16[128,1,3,2048]{3,0,2,1:T(8,128)(2,1)} %all-gather.2.cloned.1.call-done) | data formatting | bytes 3145728 | tf_op jit(solution)/shard_map/all_gather | solution.py:80
  50.8 0.2 multiply_bitcast_fusion
  51.0 1.3 copy.140
  52.3 40.8 %while.14 = (s32[]{:T(128)}, f32[128,3072]{1,0:T(8,128)S(1)}, bf16[128,16,384]{0,2,1:T(8,128)(2,1)}, bf16[384,4992]{1,0:T(8,128)(2,1)}, s32[]{:T(128)}, /*index=5*/s32[]{:T(128)}, s32[]{:T(128)}, s32[]{:T(128)}) while((s32[]{:T(128)}, f32[128,3072]{1,0:T(8,128)S(1)}, bf16[128,16,384]{0,2,1:T(8,128)(2,1)}, ...), condition=%wide.region_1.0_spmd.clone, body=%wide.region_0.0_spmd.clone.sunk | while | flops 302776320 | bytes 5603985 | solution.py:55
  52.3 2.6 %convolution_add_fusion.2 = f32[128,3072]{1,0:T(8,128)S(1)} fusion(bf16[384,4992]{1,0:T(8,128)(2,1)} %get-tuple-element.168, s32[]{:T(128)S(6)} %select_n.34, f32[128,3072]{1,0:T(8,128)S(1)} %get-tuple-element.158, pred[]{:T(512)S(6)} %compare.3, bf16[128,16,384]{0,2,1:T(8,128)(2,1)} %get-tuple-element.167, s32[]{:T(128)} %get-tuple-element.157), kind=kOutput, calls=%fused_computation.clone.1 | convolution fusion | flops 302776320 | bytes 5603845 | tf_op jit(solution)/shard_map/while/body/eval_jaxpr/dot_general | solution.py:53
  54.9 2.5 %convolution_add_fusion.2 = f32[128,3072]{1,0:T(8,128)S(1)} fusion(bf16[384,4992]{1,0:T(8,128)(2,1)} %get-tuple-element.168, s32[]{:T(128)S(6)} %select_n.34, f32[128,3072]{1,0:T(8,128)S(1)} %get-tuple-element.158, pred[]{:T(512)S(6)} %compare.3, bf16[128,16,384]{0,2,1:T(8,128)(2,1)} %get-tuple-element.167, s32[]{:T(128)} %get-tuple-element.157), kind=kOutput, calls=%fused_computation.clone.1 | convolution fusion | flops 302776320 | bytes 5603845 | tf_op jit(solution)/shard_map/while/body/eval_jaxpr/dot_general | solution.py:53
  57.5 2.5 %convolution_add_fusion.2 = f32[128,3072]{1,0:T(8,128)S(1)} fusion(bf16[384,4992]{1,0:T(8,128)(2,1)} %get-tuple-element.168, s32[]{:T(128)S(6)} %select_n.34, f32[128,3072]{1,0:T(8,128)S(1)} %get-tuple-element.158, pred[]{:T(512)S(6)} %compare.3, bf16[128,16,384]{0,2,1:T(8,128)(2,1)} %get-tuple-element.167, s32[]{:T(128)} %get-tuple-element.157), kind=kOutput, calls=%fused_computation.clone.1 | convolution fusion | flops 302776320 | bytes 5603845 | tf_op jit(solution)/shard_map/while/body/eval_jaxpr/dot_general | solution.py:53
  60.0 2.5 %convolution_add_fusion.2 = f32[128,3072]{1,0:T(8,128)S(1)} fusion(bf16[384,4992]{1,0:T(8,128)(2,1)} %get-tuple-element.168, s32[]{:T(128)S(6)} %select_n.34, f32[128,3072]{1,0:T(8,128)S(1)} %get-tuple-element.158, pred[]{:T(512)S(6)} %compare.3, bf16[128,16,384]{0,2,1:T(8,128)(2,1)} %get-tuple-element.167, s32[]{:T(128)} %get-tuple-element.157), kind=kOutput, calls=%fused_computation.clone.1 | convolution fusion | flops 302776320 | bytes 5603845 | tf_op jit(solution)/shard_map/while/body/eval_jaxpr/dot_general | solution.py:53
  62.6 2.5 %convolution_add_fusion.2 = f32[128,3072]{1,0:T(8,128)S(1)} fusion(bf16[384,4992]{1,0:T(8,128)(2,1)} %get-tuple-element.168, s32[]{:T(128)S(6)} %select_n.34, f32[128,3072]{1,0:T(8,128)S(1)} %get-tuple-element.158, pred[]{:T(512)S(6)} %compare.3, bf16[128,16,384]{0,2,1:T(8,128)(2,1)} %get-tuple-element.167, s32[]{:T(128)} %get-tuple-element.157), kind=kOutput, calls=%fused_computation.clone.1 | convolution fusion | flops 302776320 | bytes 5603845 | tf_op jit(solution)/shard_map/while/body/eval_jaxpr/dot_general | solution.py:53
  65.1 2.5 %convolution_add_fusion.2 = f32[128,3072]{1,0:T(8,128)S(1)} fusion(bf16[384,4992]{1,0:T(8,128)(2,1)} %get-tuple-element.168, s32[]{:T(128)S(6)} %select_n.34, f32[128,3072]{1,0:T(8,128)S(1)} %get-tuple-element.158, pred[]{:T(512)S(6)} %compare.3, bf16[128,16,384]{0,2,1:T(8,128)(2,1)} %get-tuple-element.167, s32[]{:T(128)} %get-tuple-element.157), kind=kOutput, calls=%fused_computation.clone.1 | convolution fusion | flops 302776320 | bytes 5603845 | tf_op jit(solution)/shard_map/while/body/eval_jaxpr/dot_general | solution.py:53
  67.7 2.5 %convolution_add_fusion.2 = f32[128,3072]{1,0:T(8,128)S(1)} fusion(bf16[384,4992]{1,0:T(8,128)(2,1)} %get-tuple-element.168, s32[]{:T(128)S(6)} %select_n.34, f32[128,3072]{1,0:T(8,128)S(1)} %get-tuple-element.158, pred[]{:T(512)S(6)} %compare.3, bf16[128,16,384]{0,2,1:T(8,128)(2,1)} %get-tuple-element.167, s32[]{:T(128)} %get-tuple-element.157), kind=kOutput, calls=%fused_computation.clone.1 | convolution fusion | flops 302776320 | bytes 5603845 | tf_op jit(solution)/shard_map/while/body/eval_jaxpr/dot_general | solution.py:53
  70.2 2.5 %convolution_add_fusion.2 = f32[128,3072]{1,0:T(8,128)S(1)} fusion(bf16[384,4992]{1,0:T(8,128)(2,1)} %get-tuple-element.168, s32[]{:T(128)S(6)} %select_n.34, f32[128,3072]{1,0:T(8,128)S(1)} %get-tuple-element.158, pred[]{:T(512)S(6)} %compare.3, bf16[128,16,384]{0,2,1:T(8,128)(2,1)} %get-tuple-element.167, s32[]{:T(128)} %get-tuple-element.157), kind=kOutput, calls=%fused_computation.clone.1 | convolution fusion | flops 302776320 | bytes 5603845 | tf_op jit(solution)/shard_map/while/body/eval_jaxpr/dot_general | solution.py:53
  72.7 2.5 %convolution_add_fusion.2 = f32[128,3072]{1,0:T(8,128)S(1)} fusion(bf16[384,4992]{1,0:T(8,128)(2,1)} %get-tuple-element.168, s32[]{:T(128)S(6)} %select_n.34, f32[128,3072]{1,0:T(8,128)S(1)} %get-tuple-element.158, pred[]{:T(512)S(6)} %compare.3, bf16[128,16,384]{0,2,1:T(8,128)(2,1)} %get-tuple-element.167, s32[]{:T(128)} %get-tuple-element.157), kind=kOutput, calls=%fused_computation.clone.1 | convolution fusion | flops 302776320 | bytes 5603845 | tf_op jit(solution)/shard_map/while/body/eval_jaxpr/dot_general | solution.py:53
  75.3 2.5 %convolution_add_fusion.2 = f32[128,3072]{1,0:T(8,128)S(1)} fusion(bf16[384,4992]{1,0:T(8,128)(2,1)} %get-tuple-element.168, s32[]{:T(128)S(6)} %select_n.34, f32[128,3072]{1,0:T(8,128)S(1)} %get-tuple-element.158, pred[]{:T(512)S(6)} %compare.3, bf16[128,16,384]{0,2,1:T(8,128)(2,1)} %get-tuple-element.167, s32[]{:T(128)} %get-tuple-element.157), kind=kOutput, calls=%fused_computation.clone.1 | convolution fusion | flops 302776320 | bytes 5603845 | tf_op jit(solution)/shard_map/while/body/eval_jaxpr/dot_general | solution.py:53
  77.8 2.5 %convolution_add_fusion.2 = f32[128,3072]{1,0:T(8,128)S(1)} fusion(bf16[384,4992]{1,0:T(8,128)(2,1)} %get-tuple-element.168, s32[]{:T(128)S(6)} %select_n.34, f32[128,3072]{1,0:T(8,128)S(1)} %get-tuple-element.158, pred[]{:T(512)S(6)} %compare.3, bf16[128,16,384]{0,2,1:T(8,128)(2,1)} %get-tuple-element.167, s32[]{:T(128)} %get-tuple-element.157), kind=kOutput, calls=%fused_computation.clone.1 | convolution fusion | flops 302776320 | bytes 5603845 | tf_op jit(solution)/shard_map/while/body/eval_jaxpr/dot_general | solution.py:53
  80.4 2.5 %convolution_add_fusion.2 = f32[128,3072]{1,0:T(8,128)S(1)} fusion(bf16[384,4992]{1,0:T(8,128)(2,1)} %get-tuple-element.168, s32[]{:T(128)S(6)} %select_n.34, f32[128,3072]{1,0:T(8,128)S(1)} %get-tuple-element.158, pred[]{:T(512)S(6)} %compare.3, bf16[128,16,384]{0,2,1:T(8,128)(2,1)} %get-tuple-element.167, s32[]{:T(128)} %get-tuple-element.157), kind=kOutput, calls=%fused_computation.clone.1 | convolution fusion | flops 302776320 | bytes 5603845 | tf_op jit(solution)/shard_map/while/body/eval_jaxpr/dot_general | solution.py:53
  82.9 2.5 %convolution_add_fusion.2 = f32[128,3072]{1,0:T(8,128)S(1)} fusion(bf16[384,4992]{1,0:T(8,128)(2,1)} %get-tuple-element.168, s32[]{:T(128)S(6)} %select_n.34, f32[128,3072]{1,0:T(8,128)S(1)} %get-tuple-element.158, pred[]{:T(512)S(6)} %compare.3, bf16[128,16,384]{0,2,1:T(8,128)(2,1)} %get-tuple-element.167, s32[]{:T(128)} %get-tuple-element.157), kind=kOutput, calls=%fused_computation.clone.1 | convolution fusion | flops 302776320 | bytes 5603845 | tf_op jit(solution)/shard_map/while/body/eval_jaxpr/dot_general | solution.py:53
  85.5 2.5 %convolution_add_fusion.2 = f32[128,3072]{1,0:T(8,128)S(1)} fusion(bf16[384,4992]{1,0:T(8,128)(2,1)} %get-tuple-element.168, s32[]{:T(128)S(6)} %select_n.34, f32[128,3072]{1,0:T(8,128)S(1)} %get-tuple-element.158, pred[]{:T(512)S(6)} %compare.3, bf16[128,16,384]{0,2,1:T(8,128)(2,1)} %get-tuple-element.167, s32[]{:T(128)} %get-tuple-element.157), kind=kOutput, calls=%fused_computation.clone.1 | convolution fusion | flops 302776320 | bytes 5603845 | tf_op jit(solution)/shard_map/while/body/eval_jaxpr/dot_general | solution.py:53
  88.0 2.5 %convolution_add_fusion.2 = f32[128,3072]{1,0:T(8,128)S(1)} fusion(bf16[384,4992]{1,0:T(8,128)(2,1)} %get-tuple-element.168, s32[]{:T(128)S(6)} %select_n.34, f32[128,3072]{1,0:T(8,128)S(1)} %get-tuple-element.158, pred[]{:T(512)S(6)} %compare.3, bf16[128,16,384]{0,2,1:T(8,128)(2,1)} %get-tuple-element.167, s32[]{:T(128)} %get-tuple-element.157), kind=kOutput, calls=%fused_computation.clone.1 | convolution fusion | flops 302776320 | bytes 5603845 | tf_op jit(solution)/shard_map/while/body/eval_jaxpr/dot_general | solution.py:53
  90.5 2.5 %convolution_add_fusion.2 = f32[128,3072]{1,0:T(8,128)S(1)} fusion(bf16[384,4992]{1,0:T(8,128)(2,1)} %get-tuple-element.168, s32[]{:T(128)S(6)} %select_n.34, f32[128,3072]{1,0:T(8,128)S(1)} %get-tuple-element.158, pred[]{:T(512)S(6)} %compare.3, bf16[128,16,384]{0,2,1:T(8,128)(2,1)} %get-tuple-element.167, s32[]{:T(128)} %get-tuple-element.157), kind=kOutput, calls=%fused_computation.clone.1 | convolution fusion | flops 302776320 | bytes 5603845 | tf_op jit(solution)/shard_map/while/body/eval_jaxpr/dot_general | solution.py:53
  93.1 0.6 multiply_reduce_fusion
  93.6 0.7 fusion.29
  94.3 1.4 multiply_multiply_fusion
  95.8 41.9 %all-reduce.2.cloned.1.call-done = f32[128,3072]{1,0:T(8,128)} async-done(((f32[128,3072]{1,0:T(8,128)}), f32[128,3072]{1,0:T(8,128)}) %all-reduce.2.cloned.1.call-update) | async-done | bytes 1572880 | tf_op jit(solution)/shard_map/psum | solution.py:92
  137.6 1.8 %constant_dynamic-slice_fusion = f32[32,3072]{1,0:T(8,128)} fusion(f32[128,3072]{1,0:T(8,128)} %all-reduce.2.cloned.1.call-done, s32[]{:T(128)S(6)} %select_n.29), kind=kLoop, calls=%fused_computation.305 | loop fusion | bytes 786436 | tf_op jit(solution)/shard_map/dynamic_slice | solution.py:93
  (122 shorter events, 11.7 us)
Async XLA Ops:
  6.5 42.3 %all-gather.2.cloned.1.call-start = ((), (), s32[]{:S(2)}) async-start(), calls=%async_computation | async-start | bytes 1966080 | tf_op jit(solution)/shard_map/all_gather | solution.py:80
  6.5 6.9 %collective-permute-start = (bf16[1,3,3072]{2,1,0:T(4,128)(2,1)}, bf16[1,3,3072]{2,1,0:T(4,128)(2,1)S(1)}, u32[]{:S(2)}, u32[]{:S(2)}) collective-permute-start(bf16[1,3,3072]{2,1,0:T(4,128)(2,1)} %param.7), channel_id=1, source_target_pairs={{1,0},{2,1},{3,2},{5,4},{6,5},{7,6},{9,8},{10,9},{11,10},{13,12},{... | collective-permute-start | bytes 55304 | tf_op jit(solution)/shard_map/ppermute | solution.py:13
  7.8 129.8 %all-reduce.2.cloned.1.call-start = ((), (), s32[]{:S(2)}) async-start(), calls=%async_computation.1 | async-start | bytes 3145728 | tf_op jit(solution)/shard_map/psum | solution.py:92
  52.3 40.8 %copy-start = (bf16[128,1,3,2048]{3,0,2,1:T(8,128)(2,1)S(1)}, bf16[128,1,3,2048]{3,0,2,1:T(8,128)(2,1)}, u32[]{:S(2)}) copy-start(bf16[128,1,3,2048]{3,0,2,1:T(8,128)(2,1)} %all-gather.2.cloned.1.call-done) | copy-start | bytes 4718596
Sparse Core Ops, SparseCore 0:
  8.9 39.9 all-gather.1
  95.9 41.6 all-reduce.1
where the time goes:
time: 147 us; the launch traced here: 146 us
  waiting for transfers between devices  63.7 us (43%)
  matrix products  40.6 us (28%)
  local copies, waits for them, and re-layouts  20.5 us (14%)
  between operations  14.6 us (10%)
  other arithmetic  5.18 us (4%)
    psum x1, waiting for transfers between devices, local(): summed = lax.psum(stacked, 'loop')  41.9 us
    dot_general x16, matrix products, add_block(): jnp.dot(weights_now, columns, preferred_element_type=jnp.float32)  40.3 us
    all_gather x1, waiting for transfers between devices, local(): panel_rows = lax.all_gather(templates, 'tgrp', axis=0, tiled=True)  18.2 us
    unnamed x129, local copies, waits for them, and re-layouts  13.1 us
    ppermute x1, waiting for transfers between devices, passed_along(): lax.ppermute(value, axis, [(source, source + steps) for source in range(i...  3.55 us
  transfers between devices with their start and end apart: 3, of which 3 were waited for; matrix products, arithmetic and copies ran while one was open for 12% of the time, Pallas kernels for 0%

commit v1 on v0

--- a/solution.py
+++ b/solution.py
@@ -89,7 +89,7 @@
     row_scale = inv_template * row_weights
     stacked = corr * inv_datas[station][None, :] * row_scale[:, None] / (3.0 * L)
     rows_here = stacked.shape[0] // lax.axis_size("loop")
-    summed = lax.psum(stacked, "loop")
+    summed = jnp.sum(lax.all_gather(stacked, "loop"), axis=0)
     return lax.dynamic_slice_in_dim(summed, loop_at * rows_here, rows_here, 0)
 
 

time: 147 us -> 153 us (1.041)
  waiting for transfers between devices: 63.7 us -> 67.2 us
  other arithmetic: 5.18 us -> 8.57 us
    all_gather x0 -> x1, waiting for transfers between devices: none -> 45.4 us  [local(): summed = jnp.sum(lax.all_gather(stacked, 'loop'), axis=0)]
    psum x1 -> x0, waiting for transfers between devices: 41.9 us -> none  [local(): summed = lax.psum(stacked, 'loop')]
    reduce_sum x0 -> x1, other arithmetic: none -> 3.39 us  [local(): summed = jnp.sum(lax.all_gather(stacked, 'loop'), axis=0)]
where the time goes in v1:
time: 153 us; the launch traced here: 152 us
  waiting for transfers between devices  67.2 us (44%)
  matrix products  40.6 us (27%)
  local copies, waits for them, and re-layouts  19.5 us (13%)
  between operations  14.6 us (10%)
  other arithmetic  8.57 us (6%)
    all_gather x1, waiting for transfers between devices, local(): summed = jnp.sum(lax.all_gather(stacked, 'loop'), axis=0)  45.4 us
    dot_general x16, matrix products, add_block(): jnp.dot(weights_now, columns, preferred_element_type=jnp.float32)  40.3 us
    all_gather x1, waiting for transfers between devices, local(): panel_rows = lax.all_gather(templates, 'tgrp', axis=0, tiled=True)  18.2 us
    unnamed x129, local copies, waits for them, and re-layouts  13.1 us
    ppermute x1, waiting for transfers between devices, passed_along(): lax.ppermute(value, axis, [(source, source + steps) for source in range(i...  3.55 us
    reduce_sum x1, other arithmetic, local(): summed = jnp.sum(lax.all_gather(stacked, 'loop'), axis=0)  3.39 us
  transfers between devices with their start and end apart: 3, of which 3 were waited for; matrix products, arithmetic and copies ran while one was open for 12% of the time, Pallas kernels for 0%

profile of v1, /device:TPU:0, one launch (start us, length us, event | category | flops | bytes accessed | tf_op | source)
XLA Modules:
  0.0 152.2 jit_solution(12872344716657278322)
XLA Ops:
  6.5 1.3 collective-permute-start
  7.9 0.7 convert_bitcast_fusion
  9.2 0.7 reduce_sum.38
  9.9 3.5 %collective-permute-done = bf16[1,3,3072]{2,1,0:T(4,128)(2,1)S(1)} collective-permute-done((bf16[1,3,3072]{2,1,0:T(4,128)(2,1)}, bf16[1,3,3072]{2,1,0:T(4,128)(2,1)S(1)}, u32[]{:S(2)}, u32[]{:S(2)}) %collective-permute-start) | collective-permute-done | bytes 18464 | tf_op jit(solution)/shard_map/ppermute | solution.py:13
  13.5 0.9 multiply_reduce_fusion.1
  14.4 0.1 constant_dynamic-update-slice_fusion.126
  15.0 0.1 constant_dynamic-update-slice_fusion.121
  15.1 0.1 constant_dynamic-update-slice_fusion.120
  15.3 0.1 constant_dynamic-update-slice_fusion.118
  15.4 0.1 constant_dynamic-update-slice_fusion.117
  15.9 0.1 constant_dynamic-update-slice_fusion.112
  16.1 0.1 constant_dynamic-update-slice_fusion.111
  16.4 0.1 constant_dynamic-update-slice_fusion.108
  16.9 0.1 constant_dynamic-update-slice_fusion.103
  17.7 0.1 constant_dynamic-update-slice_fusion.96
  19.4 0.1 constant_dynamic-update-slice_fusion.80
  21.1 0.1 constant_dynamic-update-slice_fusion.64
  24.6 0.1 constant_dynamic-update-slice_fusion.32
  28.0 0.1 constant_dynamic-update-slice_fusion
  28.1 2.2 %copy.141 = bf16[3,128,4992]{2,1,0:T(8,128)(2,1)} copy(bf16[3,128,4992]{2,0,1:T(4,128)(2,1)S(1)} %constant_dynamic-update-slice_fusion) | data formatting | bytes 7667712 | tf_op jit(solution)/shard_map/stack | solution.py:39
  30.4 0.2 fusion.4
  30.6 18.2 %all-gather.4.cloned.1.call-done = bf16[128,1,3,2048]{3,0,2,1:T(8,128)(2,1)} async-done(((bf16[32,1,3,2048]{3,0,2,1:T(8,128)(2,1)}), bf16[128,1,3,2048]{3,0,2,1:T(8,128)(2,1)}) %all-gather.4.cloned.1.call-update) | async-done | bytes 1572880 | tf_op jit(solution)/shard_map/all_gather | solution.py:80
  48.9 1.9 %copy.139 = bf16[128,1,3,2048]{0,3,2,1:T(8,128)(2,1)S(1)} copy(bf16[128,1,3,2048]{3,0,2,1:T(8,128)(2,1)} %all-gather.4.cloned.1.call-done) | data formatting | bytes 3145728 | tf_op jit(solution)/shard_map/all_gather | solution.py:80
  50.8 0.2 multiply_bitcast_fusion
  51.0 1.3 copy.140
  52.3 40.8 %while.14 = (s32[]{:T(128)}, f32[128,3072]{1,0:T(8,128)S(1)}, bf16[128,16,384]{0,2,1:T(8,128)(2,1)}, bf16[384,4992]{1,0:T(8,128)(2,1)}, s32[]{:T(128)}, /*index=5*/s32[]{:T(128)}, s32[]{:T(128)}, s32[]{:T(128)}) while((s32[]{:T(128)}, f32[128,3072]{1,0:T(8,128)S(1)}, bf16[128,16,384]{0,2,1:T(8,128)(2,1)}, ...), condition=%wide.region_1.0_spmd.clone, body=%wide.region_0.0_spmd.clone.sunk | while | flops 302776320 | bytes 5603985 | solution.py:55
  52.3 2.6 %convolution_add_fusion.2 = f32[128,3072]{1,0:T(8,128)S(1)} fusion(bf16[384,4992]{1,0:T(8,128)(2,1)} %get-tuple-element.168, s32[]{:T(128)S(6)} %select_n.34, f32[128,3072]{1,0:T(8,128)S(1)} %get-tuple-element.158, pred[]{:T(512)S(6)} %compare.3, bf16[128,16,384]{0,2,1:T(8,128)(2,1)} %get-tuple-element.167, s32[]{:T(128)} %get-tuple-element.157), kind=kOutput, calls=%fused_computation.clone.1 | convolution fusion | flops 302776320 | bytes 5603845 | tf_op jit(solution)/shard_map/while/body/eval_jaxpr/dot_general | solution.py:53
  54.9 2.5 %convolution_add_fusion.2 = f32[128,3072]{1,0:T(8,128)S(1)} fusion(bf16[384,4992]{1,0:T(8,128)(2,1)} %get-tuple-element.168, s32[]{:T(128)S(6)} %select_n.34, f32[128,3072]{1,0:T(8,128)S(1)} %get-tuple-element.158, pred[]{:T(512)S(6)} %compare.3, bf16[128,16,384]{0,2,1:T(8,128)(2,1)} %get-tuple-element.167, s32[]{:T(128)} %get-tuple-element.157), kind=kOutput, calls=%fused_computation.clone.1 | convolution fusion | flops 302776320 | bytes 5603845 | tf_op jit(solution)/shard_map/while/body/eval_jaxpr/dot_general | solution.py:53
  57.5 2.5 %convolution_add_fusion.2 = f32[128,3072]{1,0:T(8,128)S(1)} fusion(bf16[384,4992]{1,0:T(8,128)(2,1)} %get-tuple-element.168, s32[]{:T(128)S(6)} %select_n.34, f32[128,3072]{1,0:T(8,128)S(1)} %get-tuple-element.158, pred[]{:T(512)S(6)} %compare.3, bf16[128,16,384]{0,2,1:T(8,128)(2,1)} %get-tuple-element.167, s32[]{:T(128)} %get-tuple-element.157), kind=kOutput, calls=%fused_computation.clone.1 | convolution fusion | flops 302776320 | bytes 5603845 | tf_op jit(solution)/shard_map/while/body/eval_jaxpr/dot_general | solution.py:53
  60.0 2.5 %convolution_add_fusion.2 = f32[128,3072]{1,0:T(8,128)S(1)} fusion(bf16[384,4992]{1,0:T(8,128)(2,1)} %get-tuple-element.168, s32[]{:T(128)S(6)} %select_n.34, f32[128,3072]{1,0:T(8,128)S(1)} %get-tuple-element.158, pred[]{:T(512)S(6)} %compare.3, bf16[128,16,384]{0,2,1:T(8,128)(2,1)} %get-tuple-element.167, s32[]{:T(128)} %get-tuple-element.157), kind=kOutput, calls=%fused_computation.clone.1 | convolution fusion | flops 302776320 | bytes 5603845 | tf_op jit(solution)/shard_map/while/body/eval_jaxpr/dot_general | solution.py:53
  62.6 2.5 %convolution_add_fusion.2 = f32[128,3072]{1,0:T(8,128)S(1)} fusion(bf16[384,4992]{1,0:T(8,128)(2,1)} %get-tuple-element.168, s32[]{:T(128)S(6)} %select_n.34, f32[128,3072]{1,0:T(8,128)S(1)} %get-tuple-element.158, pred[]{:T(512)S(6)} %compare.3, bf16[128,16,384]{0,2,1:T(8,128)(2,1)} %get-tuple-element.167, s32[]{:T(128)} %get-tuple-element.157), kind=kOutput, calls=%fused_computation.clone.1 | convolution fusion | flops 302776320 | bytes 5603845 | tf_op jit(solution)/shard_map/while/body/eval_jaxpr/dot_general | solution.py:53
  65.1 2.5 %convolution_add_fusion.2 = f32[128,3072]{1,0:T(8,128)S(1)} fusion(bf16[384,4992]{1,0:T(8,128)(2,1)} %get-tuple-element.168, s32[]{:T(128)S(6)} %select_n.34, f32[128,3072]{1,0:T(8,128)S(1)} %get-tuple-element.158, pred[]{:T(512)S(6)} %compare.3, bf16[128,16,384]{0,2,1:T(8,128)(2,1)} %get-tuple-element.167, s32[]{:T(128)} %get-tuple-element.157), kind=kOutput, calls=%fused_computation.clone.1 | convolution fusion | flops 302776320 | bytes 5603845 | tf_op jit(solution)/shard_map/while/body/eval_jaxpr/dot_general | solution.py:53
  67.7 2.5 %convolution_add_fusion.2 = f32[128,3072]{1,0:T(8,128)S(1)} fusion(bf16[384,4992]{1,0:T(8,128)(2,1)} %get-tuple-element.168, s32[]{:T(128)S(6)} %select_n.34, f32[128,3072]{1,0:T(8,128)S(1)} %get-tuple-element.158, pred[]{:T(512)S(6)} %compare.3, bf16[128,16,384]{0,2,1:T(8,128)(2,1)} %get-tuple-element.167, s32[]{:T(128)} %get-tuple-element.157), kind=kOutput, calls=%fused_computation.clone.1 | convolution fusion | flops 302776320 | bytes 5603845 | tf_op jit(solution)/shard_map/while/body/eval_jaxpr/dot_general | solution.py:53
  70.2 2.5 %convolution_add_fusion.2 = f32[128,3072]{1,0:T(8,128)S(1)} fusion(bf16[384,4992]{1,0:T(8,128)(2,1)} %get-tuple-element.168, s32[]{:T(128)S(6)} %select_n.34, f32[128,3072]{1,0:T(8,128)S(1)} %get-tuple-element.158, pred[]{:T(512)S(6)} %compare.3, bf16[128,16,384]{0,2,1:T(8,128)(2,1)} %get-tuple-element.167, s32[]{:T(128)} %get-tuple-element.157), kind=kOutput, calls=%fused_computation.clone.1 | convolution fusion | flops 302776320 | bytes 5603845 | tf_op jit(solution)/shard_map/while/body/eval_jaxpr/dot_general | solution.py:53
  72.7 2.5 %convolution_add_fusion.2 = f32[128,3072]{1,0:T(8,128)S(1)} fusion(bf16[384,4992]{1,0:T(8,128)(2,1)} %get-tuple-element.168, s32[]{:T(128)S(6)} %select_n.34, f32[128,3072]{1,0:T(8,128)S(1)} %get-tuple-element.158, pred[]{:T(512)S(6)} %compare.3, bf16[128,16,384]{0,2,1:T(8,128)(2,1)} %get-tuple-element.167, s32[]{:T(128)} %get-tuple-element.157), kind=kOutput, calls=%fused_computation.clone.1 | convolution fusion | flops 302776320 | bytes 5603845 | tf_op jit(solution)/shard_map/while/body/eval_jaxpr/dot_general | solution.py:53
  75.3 2.5 %convolution_add_fusion.2 = f32[128,3072]{1,0:T(8,128)S(1)} fusion(bf16[384,4992]{1,0:T(8,128)(2,1)} %get-tuple-element.168, s32[]{:T(128)S(6)} %select_n.34, f32[128,3072]{1,0:T(8,128)S(1)} %get-tuple-element.158, pred[]{:T(512)S(6)} %compare.3, bf16[128,16,384]{0,2,1:T(8,128)(2,1)} %get-tuple-element.167, s32[]{:T(128)} %get-tuple-element.157), kind=kOutput, calls=%fused_computation.clone.1 | convolution fusion | flops 302776320 | bytes 5603845 | tf_op jit(solution)/shard_map/while/body/eval_jaxpr/dot_general | solution.py:53
  77.8 2.5 %convolution_add_fusion.2 = f32[128,3072]{1,0:T(8,128)S(1)} fusion(bf16[384,4992]{1,0:T(8,128)(2,1)} %get-tuple-element.168, s32[]{:T(128)S(6)} %select_n.34, f32[128,3072]{1,0:T(8,128)S(1)} %get-tuple-element.158, pred[]{:T(512)S(6)} %compare.3, bf16[128,16,384]{0,2,1:T(8,128)(2,1)} %get-tuple-element.167, s32[]{:T(128)} %get-tuple-element.157), kind=kOutput, calls=%fused_computation.clone.1 | convolution fusion | flops 302776320 | bytes 5603845 | tf_op jit(solution)/shard_map/while/body/eval_jaxpr/dot_general | solution.py:53
  80.4 2.5 %convolution_add_fusion.2 = f32[128,3072]{1,0:T(8,128)S(1)} fusion(bf16[384,4992]{1,0:T(8,128)(2,1)} %get-tuple-element.168, s32[]{:T(128)S(6)} %select_n.34, f32[128,3072]{1,0:T(8,128)S(1)} %get-tuple-element.158, pred[]{:T(512)S(6)} %compare.3, bf16[128,16,384]{0,2,1:T(8,128)(2,1)} %get-tuple-element.167, s32[]{:T(128)} %get-tuple-element.157), kind=kOutput, calls=%fused_computation.clone.1 | convolution fusion | flops 302776320 | bytes 5603845 | tf_op jit(solution)/shard_map/while/body/eval_jaxpr/dot_general | solution.py:53
  82.9 2.5 %convolution_add_fusion.2 = f32[128,3072]{1,0:T(8,128)S(1)} fusion(bf16[384,4992]{1,0:T(8,128)(2,1)} %get-tuple-element.168, s32[]{:T(128)S(6)} %select_n.34, f32[128,3072]{1,0:T(8,128)S(1)} %get-tuple-element.158, pred[]{:T(512)S(6)} %compare.3, bf16[128,16,384]{0,2,1:T(8,128)(2,1)} %get-tuple-element.167, s32[]{:T(128)} %get-tuple-element.157), kind=kOutput, calls=%fused_computation.clone.1 | convolution fusion | flops 302776320 | bytes 5603845 | tf_op jit(solution)/shard_map/while/body/eval_jaxpr/dot_general | solution.py:53
  85.5 2.5 %convolution_add_fusion.2 = f32[128,3072]{1,0:T(8,128)S(1)} fusion(bf16[384,4992]{1,0:T(8,128)(2,1)} %get-tuple-element.168, s32[]{:T(128)S(6)} %select_n.34, f32[128,3072]{1,0:T(8,128)S(1)} %get-tuple-element.158, pred[]{:T(512)S(6)} %compare.3, bf16[128,16,384]{0,2,1:T(8,128)(2,1)} %get-tuple-element.167, s32[]{:T(128)} %get-tuple-element.157), kind=kOutput, calls=%fused_computation.clone.1 | convolution fusion | flops 302776320 | bytes 5603845 | tf_op jit(solution)/shard_map/while/body/eval_jaxpr/dot_general | solution.py:53
  88.0 2.5 %convolution_add_fusion.2 = f32[128,3072]{1,0:T(8,128)S(1)} fusion(bf16[384,4992]{1,0:T(8,128)(2,1)} %get-tuple-element.168, s32[]{:T(128)S(6)} %select_n.34, f32[128,3072]{1,0:T(8,128)S(1)} %get-tuple-element.158, pred[]{:T(512)S(6)} %compare.3, bf16[128,16,384]{0,2,1:T(8,128)(2,1)} %get-tuple-element.167, s32[]{:T(128)} %get-tuple-element.157), kind=kOutput, calls=%fused_computation.clone.1 | convolution fusion | flops 302776320 | bytes 5603845 | tf_op jit(solution)/shard_map/while/body/eval_jaxpr/dot_general | solution.py:53
  90.5 2.5 %convolution_add_fusion.2 = f32[128,3072]{1,0:T(8,128)S(1)} fusion(bf16[384,4992]{1,0:T(8,128)(2,1)} %get-tuple-element.168, s32[]{:T(128)S(6)} %select_n.34, f32[128,3072]{1,0:T(8,128)S(1)} %get-tuple-element.158, pred[]{:T(512)S(6)} %compare.3, bf16[128,16,384]{0,2,1:T(8,128)(2,1)} %get-tuple-element.167, s32[]{:T(128)} %get-tuple-element.157), kind=kOutput, calls=%fused_computation.clone.1 | convolution fusion | flops 302776320 | bytes 5603845 | tf_op jit(solution)/shard_map/while/body/eval_jaxpr/dot_general | solution.py:53
  93.1 0.6 multiply_reduce_fusion
  93.6 0.7 fusion.29
  94.3 1.4 multiply_multiply_fusion
  95.8 45.4 %all-gather.6.cloned.1.call-done = f32[512,3072]{1,0:T(8,128)} async-done(((f32[128,3072]{1,0:T(8,128)}), f32[512,3072]{1,0:T(8,128)}) %all-gather.6.cloned.1.call-update) | async-done | bytes 6291472 | tf_op jit(solution)/shard_map/all_gather | solution.py:92
  141.2 3.4 %reduce_sum.39 = f32[128,3072]{1,0:T(8,128)S(1)} reduce(f32[4,128,3072]{2,1,0:T(8,128)} %bitcast.560, f32[]{:T(128)} %constant.62.clone.1), dimensions={0}, to_apply=%region_5.6 | reduce | flops 1179648 | bytes 7864324 | tf_op jit(solution)/shard_map/reduce_sum | solution.py:92
  144.6 0.8 constant_dynamic-slice_fusion
  (123 shorter events, 11.8 us)
Async XLA Ops:
  6.5 42.3 %all-gather.4.cloned.1.call-start = ((), (), s32[]{:S(2)}) async-start(), calls=%async_computation | async-start | bytes 1966080 | tf_op jit(solution)/shard_map/all_gather | solution.py:80
  6.5 6.9 %collective-permute-start = (bf16[1,3,3072]{2,1,0:T(4,128)(2,1)}, bf16[1,3,3072]{2,1,0:T(4,128)(2,1)S(1)}, u32[]{:S(2)}, u32[]{:S(2)}) collective-permute-start(bf16[1,3,3072]{2,1,0:T(4,128)(2,1)} %param.7), channel_id=1, source_target_pairs={{1,0},{2,1},{3,2},{5,4},{6,5},{7,6},{9,8},{10,9},{11,10},{13,12},{... | collective-permute-start | bytes 55304 | tf_op jit(solution)/shard_map/ppermute | solution.py:13
  7.8 133.3 %all-gather.6.cloned.1.call-start = ((), (), s32[]{:S(2)}) async-start(), calls=%async_computation.1 | async-start | bytes 7864320 | tf_op jit(solution)/shard_map/all_gather | solution.py:92
  52.3 40.8 %copy-start = (bf16[128,1,3,2048]{3,0,2,1:T(8,128)(2,1)S(1)}, bf16[128,1,3,2048]{3,0,2,1:T(8,128)(2,1)}, u32[]{:S(2)}) copy-start(bf16[128,1,3,2048]{3,0,2,1:T(8,128)(2,1)} %all-gather.4.cloned.1.call-done) | copy-start | bytes 4718596
Sparse Core Ops, SparseCore 0:
  8.9 39.9 all-gather.3
  95.9 45.2 all-gather.5
